TPU v7x, 128 devices: a whole 4x4x4 slice. The times are simulated.
128 devices in a mesh: pool: 2 (over core), grp: 4 (over y), rep: 16 (over x, z).
Axes of the slice: x: 4, y: 4, z: 4, core: 2. Of those that a mesh axis runs over, the one named last changes fastest.
Arguments:
- queries: bfloat16 [512, 8192], P('pool', 'grp'), may hold values from -64 to 64
- keys: bfloat16 [16384, 512], P('rep', 'grp'), may hold values from -7 to 7
- values: bfloat16 [16384, 512], P('rep', 'grp'), may hold values from -6 to 6
- hidden_in: bfloat16 [512, 4096], P(('pool', 'grp', 'rep')), may hold values from -4 to 4
- o_weight: bfloat16 [8192, 4096], P('grp', 'rep'), may hold values from -0.125 to 0.125
- norm_gain: bfloat16 [4096], replicated, may hold values from 0.5 to 1.5
- routes: int32 [512, 8], P(('pool', 'grp', 'rep')), may hold values from 0 to 63, as said below
- route_weights: float32 [512, 8], P(('pool', 'grp', 'rep')), may hold values from 0.02 to 0.25
- w_gate: bfloat16 [64, 4096, 1536], P(('grp', 'rep'), None, 'pool'), may hold values from -0.09375 to 0.09375
- w_up: bfloat16 [64, 4096, 1536], P(('grp', 'rep'), None, 'pool'), may hold values from -0.09375 to 0.09375
- w_down: bfloat16 [64, 1536, 4096], P(('grp', 'rep'), 'pool'), may hold values from -0.15625 to 0.15625
Outputs:
- mid_rows: bfloat16 [512, 4096], P(('pool', 'grp', 'rep'))
- expert_mix: bfloat16 [512, 4096], P(('pool', 'grp', 'rep'))
Inputs may be any that keep to these rules, and one draw needn't show every extreme that they name: `routes`: each row names 8 different experts. In the rows of one device each expert is named by no row or by exactly 2 rows, and one expert, the same on every device, is named by 2 rows on every device.
All inputs are finite; a program needn't handle non-finite values.
Results may differ from a plain program's by a relative error of at most 0.027.
Values may be sent and summed in bfloat16 or wider, within the bound.
A program may use at most 128 MiB of HBM per device.

v0:
```python
import jax
import jax.numpy as jnp
from jax import lax
from jax.sharding import PartitionSpec as P

HEAD_DIM = 128


def expert_apply(rows_in, gate_w, up_w, down_w):
    gate_proj = jnp.dot(rows_in, gate_w, preferred_element_type=jnp.float32)
    upper = jnp.dot(rows_in, up_w, preferred_element_type=jnp.float32)
    activated = (jax.nn.silu(gate_proj) * upper).astype(jnp.bfloat16)
    return jnp.dot(activated, down_w, preferred_element_type=jnp.float32)


def per_device(
    queries,
    keys,
    values,
    hidden_in,
    o_weight,
    norm_gain,
    routes,
    route_weights,
    w_gate,
    w_up,
    w_down,
):
    kv_local = keys.shape[1] // HEAD_DIM
    heads_local = queries.shape[1] // HEAD_DIM
    group_size = heads_local // kv_local
    batch_rows = queries.shape[0]
    key_span = keys.shape[0]
    per_block = min(4, group_size)
    blocks = group_size // per_block
    score_scale = HEAD_DIM ** (-0.5)
    query_blocks = jnp.moveaxis(
        queries.reshape(batch_rows, kv_local, blocks, per_block, HEAD_DIM), 2, 0
    )
    key_heads = keys.reshape(key_span, kv_local, HEAD_DIM)
    value_heads = values.reshape(key_span, kv_local, HEAD_DIM)

    def local_part(query_block):
        scores = (
            jnp.einsum("rkhd,pkd->rkhp", query_block, key_heads, preferred_element_type=jnp.float32)
            * score_scale
        )
        top_score = jnp.max(scores, axis=-1)
        exp_scores = jnp.exp(scores - top_score[..., None])
        exp_total = jnp.sum(exp_scores, axis=-1)
        weighted = jnp.einsum(
            "rkhp,pkd->rkhd",
            exp_scores.astype(jnp.bfloat16),
            value_heads,
            preferred_element_type=jnp.float32,
        )
        return (top_score, exp_total, weighted)

    top_part, total_part, value_part = lax.map(local_part, query_blocks)
    rep_size = lax.axis_size("rep")
    share = batch_rows // rep_size
    rows_heads = share * heads_local

    def by_peer(part):
        part = jnp.moveaxis(part, 0, 2)
        return part.reshape((rep_size, rows_heads) + part.shape[4:])

    stats = jnp.stack([by_peer(top_part), by_peer(total_part)], axis=1)
    payload = jnp.concatenate([by_peer(value_part), stats.reshape(rep_size, -1, HEAD_DIM)], axis=1)
    payload = lax.all_to_all(payload, "rep", split_axis=0, concat_axis=0, tiled=True)
    weighted = payload[:, :rows_heads]
    stats = payload[:, rows_heads:].reshape(rep_size, 2, rows_heads)
    joint_top = jnp.max(stats[:, 0], axis=0)
    factors = jnp.exp(stats[:, 0] - joint_top)
    exp_total = jnp.sum(stats[:, 1] * factors, axis=0)
    weighted = jnp.sum(weighted * factors[..., None], axis=0)
    attention = (weighted / exp_total[:, None]).astype(jnp.bfloat16)
    attention = lax.all_gather(
        attention.reshape(share, heads_local * HEAD_DIM), "rep", axis=0, tiled=True
    )
    head_total = lax.psum_scatter(
        jnp.dot(attention, o_weight, preferred_element_type=jnp.float32),
        "grp",
        scatter_dimension=0,
        tiled=True,
    )
    attn_proj = head_total.astype(jnp.bfloat16)
    full_rows = lax.all_to_all(attn_proj, "rep", split_axis=0, concat_axis=1, tiled=True)
    mid_rows = (hidden_in.astype(jnp.float32) + full_rows.astype(jnp.float32)).astype(jnp.bfloat16)
    mid_wide = lax.optimization_barrier(mid_rows).astype(jnp.float32)
    inverse = lax.rsqrt(jnp.mean(mid_wide * mid_wide, axis=-1, keepdims=True) + 1e-06)
    normed = (mid_wide * inverse * norm_gain.astype(jnp.float32)).astype(jnp.bfloat16)
    row_dev, topk = routes.shape
    model_width = hidden_in.shape[1]
    group_count = lax.axis_size("grp")
    rep_count = lax.axis_size("rep")
    experts = group_count * rep_count
    capacity = max(2, 2 * row_dev * topk // experts)
    flat_routes = routes.reshape(-1)
    order = jnp.arange(flat_routes.shape[0], dtype=jnp.int32)
    same_before = (flat_routes[:, None] == flat_routes[None, :]) & (order[None, :] < order[:, None])
    position = jnp.sum(same_before.astype(jnp.int32), axis=1)
    slot_index = flat_routes * capacity + position
    chooser = jnp.any(
        jnp.arange(experts * capacity, dtype=jnp.int32)[:, None, None]
        == slot_index.reshape(row_dev, topk)[None, :, :],
        axis=2,
    ).astype(jnp.bfloat16)
    outgoing = jnp.dot(chooser, normed, preferred_element_type=jnp.float32).astype(jnp.bfloat16)
    arrived = lax.all_to_all(
        outgoing.reshape(experts, capacity, model_width),
        ("grp", "rep"),
        split_axis=0,
        concat_axis=0,
        tiled=True,
    )
    sources = arrived.shape[0]
    slots_here = arrived.shape[1]
    combined = expert_apply(
        lax.all_gather(arrived.reshape(-1, model_width), "pool", axis=0, tiled=True),
        w_gate[0],
        w_up[0],
        w_down[0],
    )
    served = (
        lax.psum_scatter(combined, "pool", scatter_dimension=0, tiled=True)
        .astype(jnp.bfloat16)
        .reshape(sources, slots_here, model_width)
    )
    returned = lax.all_to_all(served, ("grp", "rep"), split_axis=0, concat_axis=0, tiled=True)
    returned = returned.reshape(-1, model_width)
    picked = jnp.take(returned, slot_index, axis=0).reshape(row_dev, topk, model_width)
    expert_mix = jnp.sum(route_weights[..., None] * picked.astype(jnp.float32), axis=1).astype(
        jnp.bfloat16
    )
    return (mid_rows, expert_mix)


def solution(mesh):
    return jax.shard_map(
        per_device,
        mesh=mesh,
        in_specs=(
            P("pool", "grp"),
            P("rep", "grp"),
            P("rep", "grp"),
            P(("pool", "grp", "rep"), None),
            P("grp", "rep"),
            P(),
            P(("pool", "grp", "rep"), None),
            P(("pool", "grp", "rep"), None),
            P(("grp", "rep"), None, "pool"),
            P(("grp", "rep"), None, "pool"),
            P(("grp", "rep"), "pool", None),
        ),
        out_specs=(P(("pool", "grp", "rep"), None), P(("pool", "grp", "rep"), None)),
        check_vma=False,
    )
```

profile of v0, /device:TPU:0, one launch (start us, length us, event | category | flops | bytes accessed | tf_op | source)
XLA Modules:
  0.0 256.5 jit_solution(1512416310897008572)
XLA Ops:
  7.3 1.6 copy.23
  8.8 17.8 %while.14 = (s32[]{:T(128)}, f32[4,256,1,4]{1,3,2,0:T(4,128)S(1)}, f32[4,256,1,4]{1,3,2,0:T(4,128)S(1)}, f32[4,256,1,4,128]{4,1,3,2,0:T(8,128)}, bf16[4,256,1,4,...) while((s32[]{:T(128)}, f32[4,256,1,4]{1,3,2,0:T(4,128)S(1)}, ...), condition=%wide.region_3.4_spmd, body=%wide.region_0.3_spmd.sunk | while | flops 545257472 | bytes 14975609 | solution.py:59
  8.8 1.8 bitcast_reduce_fusion.2
  10.7 0.9 fusion.67
  11.6 1.6 fusion.68
  13.3 1.8 bitcast_reduce_fusion.2
  15.1 0.9 fusion.67
  16.0 1.7 fusion.68
  17.7 1.8 bitcast_reduce_fusion.2
  19.5 0.9 fusion.67
  20.5 1.7 fusion.68
  22.1 1.8 bitcast_reduce_fusion.2
  23.9 0.9 fusion.67
  24.9 1.7 fusion.68
  28.2 2.9 %copy.25 = f32[256,1,4,4,128]{4,3,2,0,1:T(4,128)S(1)} copy(f32[256,1,4,4,128]{4,0,3,1,2:T(8,128)} %bitcast.21) | data formatting | bytes 4194304 | tf_op jit(solution)/shard_map/transpose | solution.py:65
  31.3 37.1 %all_to_all.28 = f32[16,260,128]{2,1,0:T(8,128)S(1)} all-to-all(f32[16,260,128]{2,1,0:T(8,128)S(1)} %pad_maximum_fusion), channel_id=1, replica_groups=mesh['pool'=2,'grp'=4,'rep'=16] {'rep'}, dimensions={0} | all-to-all | bytes 4259840 | tf_op jit(solution)/shard_map/all_to_all | solution.py:70
  70.2 40.9 %all-gather.3.cloned.1.call-done = bf16[256,2048]{1,0:T(8,128)(2,1)} async-done(((bf16[16,2048]{1,0:T(8,128)(2,1)}), bf16[256,2048]{1,0:T(8,128)(2,1)}) %all-gather.3.cloned.1.call-update) | async-done | bytes 1048592 | tf_op jit(solution)/shard_map/all_gather | solution.py:78
  111.1 2.4 fusion.55
  113.9 19.6 %reduce-scatter.3.cloned.1.call-done = f32[64,256]{1,0:T(8,128)} async-done(((f32[256,256]{1,0:T(8,128)}), f32[64,256]{1,0:T(8,128)}) %reduce-scatter.3.cloned.1.call-update) | async-done | bytes 65552 | tf_op jit(solution)/shard_map/reduce_scatter | solution.py:81
  135.0 6.9 %all-to-all-start.1 = ((bf16[16,4,256]{2,1,0:T(4,128)(2,1)}), bf16[16,4,256]{2,1,0:T(4,128)(2,1)S(1)}, u32[]{:S(2)}, u32[]{:S(2)}) async-start(bf16[16,4,256]{2,1,0:T(4,128)(2,1)} %all_to_all.20), calls=%async_computation.2 | async-start | bytes 65536 | tf_op jit(solution)/shard_map/all_to_all | solution.py:88
  142.1 7.5 %all-to-all-done.1 = bf16[16,4,256]{2,1,0:T(4,128)(2,1)S(1)} async-done(((bf16[16,4,256]{2,1,0:T(4,128)(2,1)}), bf16[16,4,256]{2,1,0:T(4,128)(2,1)S(1)}, u32[]{:S(2)}, u32[]{:S(2)}) %all-to-all-start.1) | async-done | bytes 32800 | tf_op jit(solution)/shard_map/all_to_all | solution.py:88
  151.0 20.0 %all_to_all.29 = bf16[64,2,4096]{2,1,0:T(2,128)(2,1)S(1)} all-to-all(bf16[64,2,4096]{2,1,0:T(2,128)(2,1)S(1)} %reshape.157), channel_id=1, replica_groups=mesh['pool'=2,'grp'=4,'rep'=16] {'grp','rep'}, dimensions={0} | all-to-all | bytes 2097152 | tf_op jit(solution)/shard_map/all_to_all | solution.py:110
  171.0 1.2 reshape.158
  172.5 8.8 %all-gather.5.cloned.1.call-done = bf16[256,4096]{1,0:T(8,128)(2,1)} async-done(((bf16[128,4096]{1,0:T(8,128)(2,1)}), bf16[256,4096]{1,0:T(8,128)(2,1)}) %all-gather.5.cloned.1.call-update) | async-done | bytes 2097168 | tf_op jit(solution)/shard_map/all_gather | solution.py:120
  181.3 6.2 %fusion.25 = f32[256,768]{1,0:T(8,128)} fusion(bf16[256,4096]{1,0:T(8,128)(2,1)} %all-gather.5.cloned.1.call-done, bf16[1,4096,768]{2,1,0:T(8,128)(2,1)} %param.21), kind=kOutput, calls=%fused_computation.25 | convolution fusion | flops 1610612736 | bytes 9175040 | tf_op jit(solution)/shard_map/dot_general | solution.py:10
  187.5 11.3 %fusion.21 = f32[256,4096]{1,0:T(8,128)} fusion(bf16[1,768,4096]{2,1,0:T(8,128)(2,1)} %param.23, bf16[256,4096]{1,0:T(8,128)(2,1)S(1)} %copy-done.7, bf16[1,4096,768]{2,1,0:T(8,128)(2,1)} %param.22, f32[256,768]{1,0:T(8,128)} %fusion.25), kind=kOutput, calls=%fused_computation.21 | convolution fusion | flops 3222405120 | bytes 19660800 | tf_op jit(solution)/shard_map/dot_general | solution.py:13
  198.9 16.4 %reduce-scatter.5.cloned.1.call-done = f32[128,4096]{1,0:T(8,128)} async-done(((f32[256,4096]{1,0:T(8,128)}), f32[128,4096]{1,0:T(8,128)}) %reduce-scatter.5.cloned.1.call-update) | async-done | bytes 2097168 | tf_op jit(solution)/shard_map/reduce_scatter | solution.py:126
  215.2 1.7 convert_element_type.66
  217.0 1.5 reshape.159
  218.5 10.4 %all-to-all-start.3 = ((bf16[64,2,4096]{2,1,0:T(2,128)(2,1)}), bf16[64,2,4096]{2,1,0:T(2,128)(2,1)S(1)}, u32[]{:S(2)}, u32[]{:S(2)}) async-start(bf16[64,2,4096]{2,1,0:T(2,128)(2,1)} %reshape.159), calls=%async_computation.5 | async-start | bytes 2097152 | tf_op jit(solution)/shard_map/all_to_all | solution.py:130
  229.0 18.9 %all-to-all-done.3 = bf16[64,2,4096]{2,1,0:T(2,128)(2,1)S(1)} async-done(((bf16[64,2,4096]{2,1,0:T(2,128)(2,1)}), bf16[64,2,4096]{2,1,0:T(2,128)(2,1)S(1)}, u32[]{:S(2)}, u32[]{:S(2)}) %all-to-all-start.3) | async-done | bytes 1048608 | tf_op jit(solution)/shard_map/all_to_all | solution.py:130
  249.1 0.9 multiply_reduce_fusion
  (74 shorter events, 8.5 us)
Async XLA Ops:
  7.2 104.0 %copy-start = (bf16[2048,256]{1,0:T(8,128)(2,1)S(1)}, bf16[2048,256]{1,0:T(8,128)(2,1)}, u32[]{:S(2)}) copy-start(bf16[2048,256]{1,0:T(8,128)(2,1)} %param.17) | copy-start | bytes 3145732
  7.2 103.9 %all-gather.3.cloned.1.call-start = ((), (), s32[]{:S(2)}) async-start(), calls=%async_computation.6 | async-start | bytes 1114112 | tf_op jit(solution)/shard_map/all_gather | solution.py:78
  8.8 2.8 %copy-start.1 = (bf16[1024,1,128]{2,0,1:T(8,128)(2,1)S(1)}, bf16[1024,1,128]{2,0,1:T(8,128)(2,1)}, u32[]{:S(2)}) copy-start(bf16[1024,1,128]{2,0,1:T(8,128)(2,1)} %get-tuple-element.156) | copy-start | bytes 786436 | tf_op jit(solution)/shard_map/while
  13.3 2.8 %copy-start.1 = (bf16[1024,1,128]{2,0,1:T(8,128)(2,1)S(1)}, bf16[1024,1,128]{2,0,1:T(8,128)(2,1)}, u32[]{:S(2)}) copy-start(bf16[1024,1,128]{2,0,1:T(8,128)(2,1)} %get-tuple-element.156) | copy-start | bytes 786436 | tf_op jit(solution)/shard_map/while
  17.7 2.8 %copy-start.1 = (bf16[1024,1,128]{2,0,1:T(8,128)(2,1)S(1)}, bf16[1024,1,128]{2,0,1:T(8,128)(2,1)}, u32[]{:S(2)}) copy-start(bf16[1024,1,128]{2,0,1:T(8,128)(2,1)} %get-tuple-element.156) | copy-start | bytes 786436 | tf_op jit(solution)/shard_map/while
  22.1 2.8 %copy-start.1 = (bf16[1024,1,128]{2,0,1:T(8,128)(2,1)S(1)}, bf16[1024,1,128]{2,0,1:T(8,128)(2,1)}, u32[]{:S(2)}) copy-start(bf16[1024,1,128]{2,0,1:T(8,128)(2,1)} %get-tuple-element.156) | copy-start | bytes 786436 | tf_op jit(solution)/shard_map/while
  31.3 82.3 %copy-start.4 = (s32[4,8]{1,0:T(4,128)S(1)}, s32[4,8]{1,0:T(4,128)}, u32[]{:S(2)}) copy-start(s32[4,8]{1,0:T(4,128)} %param.19) | copy-start | bytes 388
  31.3 110.8 %copy-start.5 = (bf16[4096]{0:T(1024)(128)(2,1)S(1)}, bf16[4096]{0:T(1024)(128)(2,1)}, u32[]{:S(2)}) copy-start(bf16[4096]{0:T(1024)(128)(2,1)} %param.18) | copy-start | bytes 24580
  68.4 81.2 %copy-start.3 = (bf16[4,4096]{1,0:T(4,128)(2,1)S(1)}, bf16[4,4096]{1,0:T(4,128)(2,1)}, u32[]{:S(2)}) copy-start(bf16[4,4096]{1,0:T(4,128)(2,1)} %param.16) | copy-start | bytes 98308
  70.2 63.4 %reduce-scatter.3.cloned.1.call-start = ((), (), s32[]{:S(2)}) async-start(), calls=%async_computation.7 | async-start | bytes 327680 | tf_op jit(solution)/shard_map/reduce_scatter | solution.py:81
  135.0 14.6 %all-to-all-start.1 = ((bf16[16,4,256]{2,1,0:T(4,128)(2,1)}), bf16[16,4,256]{2,1,0:T(4,128)(2,1)S(1)}, u32[]{:S(2)}, u32[]{:S(2)}) async-start(bf16[16,4,256]{2,1,0:T(4,128)(2,1)} %all_to_all.20), calls=%async_computation.2 | async-start | bytes 65536 | tf_op jit(solution)/shard_map/all_to_all | solution.py:88
  142.0 39.4 %all-gather.5.cloned.1.call-start = ((), (), s32[]{:S(2)}) async-start(), calls=%async_computation.8 | async-start | bytes 3145728 | tf_op jit(solution)/shard_map/all_gather | solution.py:120
  149.6 22.6 %copy-start.2 = (bf16[4,4096]{1,0:T(4,128)(2,1)}, bf16[4,4096]{1,0:T(4,128)(2,1)S(1)}, u32[]{:S(2)}) copy-start(bf16[4,4096]{1,0:T(4,128)(2,1)S(1)} %add_convert_fusion) | copy-start | bytes 98308
  172.3 43.0 %reduce-scatter.5.cloned.1.call-start = ((), (), s32[]{:S(2)}) async-start(), calls=%async_computation.9 | async-start | bytes 6291456 | tf_op jit(solution)/shard_map/reduce_scatter | solution.py:126
  181.3 6.2 %copy-start.7 = (bf16[256,4096]{1,0:T(8,128)(2,1)S(1)}, bf16[256,4096]{1,0:T(8,128)(2,1)}, u32[]{:S(2)}) copy-start(bf16[256,4096]{1,0:T(8,128)(2,1)} %all-gather.5.cloned.1.call-done) | copy-start | bytes 6291460
  217.0 32.1 %copy-start.6 = (f32[4,8]{1,0:T(4,128)S(1)}, f32[4,8]{1,0:T(4,128)}, u32[]{:S(2)}) copy-start(f32[4,8]{1,0:T(4,128)} %param.20) | copy-start | bytes 388
  218.5 29.4 %all-to-all-start.3 = ((bf16[64,2,4096]{2,1,0:T(2,128)(2,1)}), bf16[64,2,4096]{2,1,0:T(2,128)(2,1)S(1)}, u32[]{:S(2)}, u32[]{:S(2)}) async-start(bf16[64,2,4096]{2,1,0:T(2,128)(2,1)} %reshape.159), calls=%async_computation.5 | async-start | bytes 2097152 | tf_op jit(solution)/shard_map/all_to_all | solution.py:130
Sparse Core Ops, SparseCore 0:
  70.3 40.8 all-gather.2
  113.6 19.8 reduce-scatter.2
  172.4 8.9 all-gather.4
  199.0 16.1 reduce-scatter.4
where the time goes:
time: 257 us; the launch traced here: 256 us
  waiting for transfers between devices  112 us (44%)
  blocking collectives  57.1 us (22%)
  matrix products  34.3 us (13%)
  starting transfers between devices  17.7 us (7%)
  between operations  14 us (5%)
  local copies, waits for them, and re-layouts  11.9 us (5%)
  other arithmetic  9.24 us (4%)
    all_gather x1, waiting for transfers between devices, per_device(): lax.all_gather(attention.reshape(share, heads_local * HEAD_DIM), 'rep', a...  40.9 us
    all_to_all x1, blocking collectives, per_device(): lax.all_to_all(payload, 'rep', split_axis=0, concat_axis=0, tiled=True)  37.1 us
    all_to_all x1, blocking collectives, per_device(): lax.all_to_all(outgoing.reshape(experts, capacity, model_width), ('grp',...  20 us
    reduce_scatter x1, waiting for transfers between devices, per_device(): lax.psum_scatter(jnp.dot(attention, o_weight, preferred_element_type=jnp....  19.6 us
    all_to_all x1, waiting for transfers between devices, per_device(): lax.all_to_all(served, ('grp', 'rep'), split_axis=0, concat_axis=0, tiled...  18.9 us
    reduce_scatter x1, waiting for transfers between devices, per_device(): lax.psum_scatter(combined, 'pool', scatter_dimension=0, tiled=True)  16.4 us
    dot_general x1, matrix products, expert_apply(): return jnp.dot(activated, down_w, preferred_element_type=jnp.float32)  11.3 us
    all_to_all x1, starting transfers between devices, per_device(): lax.all_to_all(served, ('grp', 'rep'), split_axis=0, concat_axis=0, tiled...  10.4 us
  transfers between devices with their start and end apart: 6, of which 6 were waited for; matrix products, arithmetic and copies ran while one was open for 0% of the time, Pallas kernels for 0%

commit v1 on v0

--- a/solution.py
+++ b/solution.py
@@ -75,9 +75,23 @@
     exp_total = jnp.sum(stats[:, 1] * factors, axis=0)
     weighted = jnp.sum(weighted * factors[..., None], axis=0)
     attention = (weighted / exp_total[:, None]).astype(jnp.bfloat16)
-    attention = lax.all_gather(
-        attention.reshape(share, heads_local * HEAD_DIM), "rep", axis=0, tiled=True
+    array = attention.reshape(share, heads_local * HEAD_DIM)
+    ways, here, step = (lax.axis_size("rep"), lax.axis_index("rep"), array.shape[0])
+    lengths = [n * ways if d == 0 else n for d, n in enumerate(array.shape)]
+    attention = lax.dynamic_update_slice_in_dim(
+        jnp.zeros(lengths, array.dtype), array, here * step, axis=0
     )
+    going_up = going_down = array
+    for far in range(1, ways // 2 + 1):
+        going_up = lax.ppermute(going_up, "rep", [(d, (d + 1) % ways) for d in range(ways)])
+        attention = lax.dynamic_update_slice_in_dim(
+            attention, going_up, (here - far) % ways * step, axis=0
+        )
+        if 2 * far < ways:
+            going_down = lax.ppermute(going_down, "rep", [(d, (d - 1) % ways) for d in range(ways)])
+            attention = lax.dynamic_update_slice_in_dim(
+                attention, going_down, (here + far) % ways * step, axis=0
+            )
     head_total = lax.psum_scatter(
         jnp.dot(attention, o_weight, preferred_element_type=jnp.float32),
         "grp",

time: 257 us -> 276 us (1.074)
  starting transfers between devices: 17.7 us -> 64 us
  blocking collectives: 57.1 us -> 20 us
  waiting for transfers between devices: 112 us -> 122 us
    all_gather x1 -> x0, waiting for transfers between devices: 40.9 us -> none  [per_device(): lax.all_gather(attention.reshape(share, heads_local * HEAD_DIM), 'rep', a...]
    ppermute x0 -> x15, starting transfers between devices: none -> 38.6 us  [the longest x7 38 us: per_device(): lax.ppermute(going_down, 'rep', [(d, (d - 1) % ways) for d in range(ways)])]
    all_to_all x1 -> x0, blocking collectives: 37.1 us -> none  [per_device(): lax.all_to_all(payload, 'rep', split_axis=0, concat_axis=0, tiled=True)]
    all_to_all x0 -> x1, waiting for transfers between devices: none -> 31.1 us  [per_device(): lax.all_to_all(payload, 'rep', split_axis=0, concat_axis=0, tiled=True)]
    ppermute x0 -> x15, waiting for transfers between devices: none -> 22.3 us  [the longest x8 22.3 us: per_device(): lax.ppermute(going_up, 'rep', [(d, (d + 1) % ways) for d in range(ways)])]
    all_to_all x0 -> x1, starting transfers between devices: none -> 7.96 us  [per_device(): lax.all_to_all(payload, 'rep', split_axis=0, concat_axis=0, tiled=True)]
    reduce_scatter x1, waiting for transfers between devices: 19.6 us -> 16.8 us  [per_device(): lax.psum_scatter(jnp.dot(attention, o_weight, preferred_element_type=jnp....]
  transfers between devices with their start and end apart: 6 -> 21, of which waited for: 6 -> 14; matrix products, arithmetic and copies ran while one was open for 0% -> 0% of each run, Pallas kernels for 0% -> 0%
where the time goes in v1:
time: 276 us; the launch traced here: 275 us
  waiting for transfers between devices  122 us (44%)
  starting transfers between devices  64 us (23%)
  matrix products  33.1 us (12%)
  blocking collectives  20 us (7%)
  between operations  14.1 us (5%)
  local copies, waits for them, and re-layouts  12.1 us (4%)
  other arithmetic  9.97 us (4%)
    ppermute x7, starting transfers between devices, per_device(): lax.ppermute(going_down, 'rep', [(d, (d - 1) % ways) for d in range(ways)])  38 us
    all_to_all x1, waiting for transfers between devices, per_device(): lax.all_to_all(payload, 'rep', split_axis=0, concat_axis=0, tiled=True)  31.1 us
    ppermute x8, waiting for transfers between devices, per_device(): lax.ppermute(going_up, 'rep', [(d, (d + 1) % ways) for d in range(ways)])  22.3 us
    all_to_all x1, blocking collectives, per_device(): lax.all_to_all(outgoing.reshape(experts, capacity, model_width), ('grp',...  20 us
    all_to_all x1, waiting for transfers between devices, per_device(): lax.all_to_all(served, ('grp', 'rep'), split_axis=0, concat_axis=0, tiled...  18.9 us
    reduce_scatter x1, waiting for transfers between devices, per_device(): lax.psum_scatter(jnp.dot(attention, o_weight, preferred_element_type=jnp....  16.8 us
    reduce_scatter x1, waiting for transfers between devices, per_device(): lax.psum_scatter(combined, 'pool', scatter_dimension=0, tiled=True)  16.4 us
    dot_general x1, matrix products, expert_apply(): return jnp.dot(activated, down_w, preferred_element_type=jnp.float32)  11.3 us
  transfers between devices with their start and end apart: 21, of which 14 were waited for; matrix products, arithmetic and copies ran while one was open for 0% of the time, Pallas kernels for 0%

profile of v1, /device:TPU:0, one launch (start us, length us, event | category | flops | bytes accessed | tf_op | source)
XLA Modules:
  0.0 275.5 jit_solution(17222109291386911689)
XLA Ops:
  8.8 17.7 %while.14 = (s32[]{:T(128)}, f32[4,256,1,4]{1,3,2,0:T(4,128)S(1)}, f32[4,256,1,4]{1,3,2,0:T(4,128)S(1)}, f32[4,256,1,4,128]{4,1,3,2,0:T(8,128)}, bf16[4,256,1,4,...) while((s32[]{:T(128)}, f32[4,256,1,4]{1,3,2,0:T(4,128)S(1)}, ...), condition=%wide.region_3.4_spmd, body=%wide.region_0.3_spmd.sunk | while | flops 545257472 | bytes 14975609 | solution.py:59
  13.2 1.8 bitcast_reduce_fusion.2
  17.6 1.8 bitcast_reduce_fusion.2
  22.1 1.8 bitcast_reduce_fusion.2
  28.1 2.9 %copy.25 = f32[256,1,4,4,128]{4,3,2,0,1:T(4,128)S(1)} copy(f32[256,1,4,4,128]{4,0,3,1,2:T(8,128)} %bitcast.21) | data formatting | bytes 4194304 | tf_op jit(solution)/shard_map/transpose | solution.py:65
  32.6 8.0 %all-to-all-start = ((f32[16,260,128]{2,1,0:T(8,128)}), f32[16,260,128]{2,1,0:T(8,128)S(1)}, u32[]{:S(2)}, u32[]{:S(2)}) async-start(f32[16,260,128]{2,1,0:T(8,128)} %pad_maximum_fusion), calls=%async_computation | async-start | bytes 4325376 | tf_op jit(solution)/shard_map/all_to_all | solution.py:70
  40.6 31.1 %all-to-all-done = f32[16,260,128]{2,1,0:T(8,128)S(1)} async-done(((f32[16,260,128]{2,1,0:T(8,128)}), f32[16,260,128]{2,1,0:T(8,128)S(1)}, u32[]{:S(2)}, u32[]{:S(2)}) %all-to-all-start) | async-done | bytes 2129952 | tf_op jit(solution)/shard_map/all_to_all | solution.py:70
  73.6 4.8 %collective-permute-start.1 = (bf16[16,2048]{1,0:T(8,128)(2,1)S(1)}, bf16[16,2048]{1,0:T(8,128)(2,1)S(1)}, u32[]{:S(2)}, u32[]{:S(2)}) collective-permute-start(bf16[16,2048]{1,0:T(8,128)(2,1)S(1)} %get-tuple-element.75), channel_id=1, source_target_pairs={{0,15},{1,0},{2,1},{3,2},{4,3},{5,4},{6,5},{7,6},{8,7},{9,8},{10,9... | collective-permute-start | bytes 196616 | tf_op jit(solution)/shard_map/ppermute | solution.py:91
  78.4 2.2 collective-permute-done
  80.7 5.3 %collective-permute-start.3 = (bf16[16,2048]{1,0:T(8,128)(2,1)S(1)}, bf16[16,2048]{1,0:T(8,128)(2,1)S(1)}, u32[]{:S(2)}, u32[]{:S(2)}) collective-permute-start(bf16[16,2048]{1,0:T(8,128)(2,1)S(1)} %collective-permute-done.1), channel_id=1, source_target_pairs={{0,15},{1,0},{2,1},{3,2},{4,3},{5,4},{6,5},{7,6},{8,7},{9,8},{10,9... | collective-permute-start | bytes 196616 | tf_op jit(solution)/shard_map/ppermute | solution.py:91
  86.0 2.2 collective-permute-done.2
  88.3 5.3 %collective-permute-start.5 = (bf16[16,2048]{1,0:T(8,128)(2,1)S(1)}, bf16[16,2048]{1,0:T(8,128)(2,1)S(1)}, u32[]{:S(2)}, u32[]{:S(2)}) collective-permute-start(bf16[16,2048]{1,0:T(8,128)(2,1)S(1)} %collective-permute-done.3), channel_id=1, source_target_pairs={{0,15},{1,0},{2,1},{3,2},{4,3},{5,4},{6,5},{7,6},{8,7},{9,8},{10,9... | collective-permute-start | bytes 196616 | tf_op jit(solution)/shard_map/ppermute | solution.py:91
  93.6 2.6 collective-permute-done.4
  96.2 5.6 %collective-permute-start.7 = (bf16[16,2048]{1,0:T(8,128)(2,1)S(1)}, bf16[16,2048]{1,0:T(8,128)(2,1)S(1)}, u32[]{:S(2)}, u32[]{:S(2)}) collective-permute-start(bf16[16,2048]{1,0:T(8,128)(2,1)S(1)} %collective-permute-done.5), channel_id=1, source_target_pairs={{0,15},{1,0},{2,1},{3,2},{4,3},{5,4},{6,5},{7,6},{8,7},{9,8},{10,9... | collective-permute-start | bytes 196616 | tf_op jit(solution)/shard_map/ppermute | solution.py:91
  101.9 1.9 collective-permute-done.6
  103.8 5.6 %collective-permute-start.9 = (bf16[16,2048]{1,0:T(8,128)(2,1)S(1)}, bf16[16,2048]{1,0:T(8,128)(2,1)S(1)}, u32[]{:S(2)}, u32[]{:S(2)}) collective-permute-start(bf16[16,2048]{1,0:T(8,128)(2,1)S(1)} %collective-permute-done.7), channel_id=1, source_target_pairs={{0,15},{1,0},{2,1},{3,2},{4,3},{5,4},{6,5},{7,6},{8,7},{9,8},{10,9... | collective-permute-start | bytes 196616 | tf_op jit(solution)/shard_map/ppermute | solution.py:91
  109.4 1.9 collective-permute-done.8
  111.4 5.6 %collective-permute-start.11 = (bf16[16,2048]{1,0:T(8,128)(2,1)S(1)}, bf16[16,2048]{1,0:T(8,128)(2,1)S(1)}, u32[]{:S(2)}, u32[]{:S(2)}) collective-permute-start(bf16[16,2048]{1,0:T(8,128)(2,1)S(1)} %collective-permute-done.9), channel_id=1, source_target_pairs={{0,15},{1,0},{2,1},{3,2},{4,3},{5,4},{6,5},{7,6},{8,7},{9,8},{10,9... | collective-permute-start | bytes 196616 | tf_op jit(solution)/shard_map/ppermute | solution.py:91
  117.0 1.9 collective-permute-done.10
  119.0 5.6 %collective-permute-start.13 = (bf16[16,2048]{1,0:T(8,128)(2,1)S(1)}, bf16[16,2048]{1,0:T(8,128)(2,1)S(1)}, u32[]{:S(2)}, u32[]{:S(2)}) collective-permute-start(bf16[16,2048]{1,0:T(8,128)(2,1)S(1)} %collective-permute-done.11), channel_id=1, source_target_pairs={{0,15},{1,0},{2,1},{3,2},{4,3},{5,4},{6,5},{7,6},{8,7},{9,8},{10,9... | collective-permute-start | bytes 196616 | tf_op jit(solution)/shard_map/ppermute | solution.py:91
  124.6 1.9 collective-permute-done.12
  126.6 7.5 %collective-permute-done.14 = bf16[16,2048]{1,0:T(8,128)(2,1)S(1)} collective-permute-done((bf16[16,2048]{1,0:T(8,128)(2,1)S(1)}, bf16[16,2048]{1,0:T(8,128)(2,1)S(1)}, u32[]{:S(2)}, u32[]{:S(2)}) %collective-permute-start.14) | collective-permute-done | bytes 65568 | tf_op jit(solution)/shard_map/ppermute | solution.py:86
  135.7 16.8 %reduce-scatter.3.cloned.1.call-done = f32[64,256]{1,0:T(8,128)} async-done(((f32[256,256]{1,0:T(8,128)}), f32[64,256]{1,0:T(8,128)}) %reduce-scatter.3.cloned.1.call-update) | async-done | bytes 65552 | tf_op jit(solution)/shard_map/reduce_scatter | solution.py:95
  154.0 6.9 %all-to-all-start.1 = ((bf16[16,4,256]{2,1,0:T(4,128)(2,1)}), bf16[16,4,256]{2,1,0:T(4,128)(2,1)S(1)}, u32[]{:S(2)}, u32[]{:S(2)}) async-start(bf16[16,4,256]{2,1,0:T(4,128)(2,1)} %all_to_all.20), calls=%async_computation.2 | async-start | bytes 65536 | tf_op jit(solution)/shard_map/all_to_all | solution.py:102
  161.1 7.5 %all-to-all-done.1 = bf16[16,4,256]{2,1,0:T(4,128)(2,1)S(1)} async-done(((bf16[16,4,256]{2,1,0:T(4,128)(2,1)}), bf16[16,4,256]{2,1,0:T(4,128)(2,1)S(1)}, u32[]{:S(2)}, u32[]{:S(2)}) %all-to-all-start.1) | async-done | bytes 32800 | tf_op jit(solution)/shard_map/all_to_all | solution.py:102
  170.0 20.0 %all_to_all.28 = bf16[64,2,4096]{2,1,0:T(2,128)(2,1)S(1)} all-to-all(bf16[64,2,4096]{2,1,0:T(2,128)(2,1)S(1)} %reshape.157), channel_id=1, replica_groups=mesh['pool'=2,'grp'=4,'rep'=16] {'grp','rep'}, dimensions={0} | all-to-all | bytes 2097152 | tf_op jit(solution)/shard_map/all_to_all | solution.py:124
  191.3 9.0 %all-gather.2.cloned.1.call-done = bf16[256,4096]{1,0:T(8,128)(2,1)} async-done(((bf16[128,4096]{1,0:T(8,128)(2,1)}), bf16[256,4096]{1,0:T(8,128)(2,1)}) %all-gather.2.cloned.1.call-update) | async-done | bytes 2097168 | tf_op jit(solution)/shard_map/all_gather | solution.py:134
  200.3 6.2 %fusion.25 = f32[256,768]{1,0:T(8,128)} fusion(bf16[256,4096]{1,0:T(8,128)(2,1)} %all-gather.2.cloned.1.call-done, bf16[1,4096,768]{2,1,0:T(8,128)(2,1)} %param.21), kind=kOutput, calls=%fused_computation.25 | convolution fusion | flops 1610612736 | bytes 9175040 | tf_op jit(solution)/shard_map/dot_general | solution.py:10
  206.5 11.3 %fusion.21 = f32[256,4096]{1,0:T(8,128)} fusion(bf16[1,768,4096]{2,1,0:T(8,128)(2,1)} %param.23, bf16[256,4096]{1,0:T(8,128)(2,1)S(1)} %copy-done.7, bf16[1,4096,768]{2,1,0:T(8,128)(2,1)} %param.22, f32[256,768]{1,0:T(8,128)} %fusion.25), kind=kOutput, calls=%fused_computation.21 | convolution fusion | flops 3222405120 | bytes 19660800 | tf_op jit(solution)/shard_map/dot_general | solution.py:13
  217.9 16.4 %reduce-scatter.5.cloned.1.call-done = f32[128,4096]{1,0:T(8,128)} async-done(((f32[256,4096]{1,0:T(8,128)}), f32[128,4096]{1,0:T(8,128)}) %reduce-scatter.5.cloned.1.call-update) | async-done | bytes 2097168 | tf_op jit(solution)/shard_map/reduce_scatter | solution.py:140
  237.5 10.4 %all-to-all-start.3 = ((bf16[64,2,4096]{2,1,0:T(2,128)(2,1)}), bf16[64,2,4096]{2,1,0:T(2,128)(2,1)S(1)}, u32[]{:S(2)}, u32[]{:S(2)}) async-start(bf16[64,2,4096]{2,1,0:T(2,128)(2,1)} %reshape.159), calls=%async_computation.5 | async-start | bytes 2097152 | tf_op jit(solution)/shard_map/all_to_all | solution.py:144
  248.0 18.9 %all-to-all-done.3 = bf16[64,2,4096]{2,1,0:T(2,128)(2,1)S(1)} async-done(((bf16[64,2,4096]{2,1,0:T(2,128)(2,1)}), bf16[64,2,4096]{2,1,0:T(2,128)(2,1)S(1)}, u32[]{:S(2)}, u32[]{:S(2)}) %all-to-all-start.3) | async-done | bytes 1048608 | tf_op jit(solution)/shard_map/all_to_all | solution.py:144
  (118 shorter events, 30.1 us)
Async XLA Ops:
  7.2 127.0 %copy-start = (bf16[2048,256]{1,0:T(8,128)(2,1)S(1)}, bf16[2048,256]{1,0:T(8,128)(2,1)}, u32[]{:S(2)}) copy-start(bf16[2048,256]{1,0:T(8,128)(2,1)} %param.17) | copy-start | bytes 3145732
  8.8 2.8 %copy-start.1 = (bf16[1024,1,128]{2,0,1:T(8,128)(2,1)S(1)}, bf16[1024,1,128]{2,0,1:T(8,128)(2,1)}, u32[]{:S(2)}) copy-start(bf16[1024,1,128]{2,0,1:T(8,128)(2,1)} %get-tuple-element.158) | copy-start | bytes 786436 | tf_op jit(solution)/shard_map/while
  13.2 2.8 %copy-start.1 = (bf16[1024,1,128]{2,0,1:T(8,128)(2,1)S(1)}, bf16[1024,1,128]{2,0,1:T(8,128)(2,1)}, u32[]{:S(2)}) copy-start(bf16[1024,1,128]{2,0,1:T(8,128)(2,1)} %get-tuple-element.158) | copy-start | bytes 786436 | tf_op jit(solution)/shard_map/while
  17.6 2.8 %copy-start.1 = (bf16[1024,1,128]{2,0,1:T(8,128)(2,1)S(1)}, bf16[1024,1,128]{2,0,1:T(8,128)(2,1)}, u32[]{:S(2)}) copy-start(bf16[1024,1,128]{2,0,1:T(8,128)(2,1)} %get-tuple-element.158) | copy-start | bytes 786436 | tf_op jit(solution)/shard_map/while
  22.1 2.8 %copy-start.1 = (bf16[1024,1,128]{2,0,1:T(8,128)(2,1)S(1)}, bf16[1024,1,128]{2,0,1:T(8,128)(2,1)}, u32[]{:S(2)}) copy-start(bf16[1024,1,128]{2,0,1:T(8,128)(2,1)} %get-tuple-element.158) | copy-start | bytes 786436 | tf_op jit(solution)/shard_map/while
  32.6 39.2 %all-to-all-start = ((f32[16,260,128]{2,1,0:T(8,128)}), f32[16,260,128]{2,1,0:T(8,128)S(1)}, u32[]{:S(2)}, u32[]{:S(2)}) async-start(f32[16,260,128]{2,1,0:T(8,128)} %pad_maximum_fusion), calls=%async_computation | async-start | bytes 4325376 | tf_op jit(solution)/shard_map/all_to_all | solution.py:70
  40.5 112.0 %reduce-scatter.3.cloned.1.call-start = ((), (), s32[]{:S(2)}) async-start(), calls=%async_computation.6 | async-start | bytes 327680 | tf_op jit(solution)/shard_map/reduce_scatter | solution.py:95
  71.9 63.5 %copy-start.4 = (s32[4,8]{1,0:T(4,128)S(1)}, s32[4,8]{1,0:T(4,128)}, u32[]{:S(2)}) copy-start(s32[4,8]{1,0:T(4,128)} %param.19) | copy-start | bytes 388
  71.9 89.2 %copy-start.5 = (bf16[4096]{0:T(1024)(128)(2,1)S(1)}, bf16[4096]{0:T(1024)(128)(2,1)}, u32[]{:S(2)}) copy-start(bf16[4096]{0:T(1024)(128)(2,1)} %param.18) | copy-start | bytes 24580
  72.6 96.0 %copy-start.3 = (bf16[4,4096]{1,0:T(4,128)(2,1)S(1)}, bf16[4,4096]{1,0:T(4,128)(2,1)}, u32[]{:S(2)}) copy-start(bf16[4,4096]{1,0:T(4,128)(2,1)} %param.16) | copy-start | bytes 98308
  73.0 7.7 %collective-permute-start = (bf16[16,2048]{1,0:T(8,128)(2,1)S(1)}, bf16[16,2048]{1,0:T(8,128)(2,1)S(1)}, u32[]{:S(2)}, u32[]{:S(2)}) collective-permute-start(bf16[16,2048]{1,0:T(8,128)(2,1)S(1)} %get-tuple-element.75), channel_id=1, source_target_pairs={{0,1},{1,2},{2,3},{3,4},{4,5},{5,6},{6,7},{7,8},{8,9},{9,10},{10,1... | collective-permute-start | bytes 196616 | tf_op jit(solution)/shard_map/ppermute | solution.py:86
  73.6 7.0 %collective-permute-start.1 = (bf16[16,2048]{1,0:T(8,128)(2,1)S(1)}, bf16[16,2048]{1,0:T(8,128)(2,1)S(1)}, u32[]{:S(2)}, u32[]{:S(2)}) collective-permute-start(bf16[16,2048]{1,0:T(8,128)(2,1)S(1)} %get-tuple-element.75), channel_id=1, source_target_pairs={{0,15},{1,0},{2,1},{3,2},{4,3},{5,4},{6,5},{7,6},{8,7},{9,8},{10,9... | collective-permute-start | bytes 196616 | tf_op jit(solution)/shard_map/ppermute | solution.py:91
  80.7 7.6 %collective-permute-start.2 = (bf16[16,2048]{1,0:T(8,128)(2,1)S(1)}, bf16[16,2048]{1,0:T(8,128)(2,1)S(1)}, u32[]{:S(2)}, u32[]{:S(2)}) collective-permute-start(bf16[16,2048]{1,0:T(8,128)(2,1)S(1)} %collective-permute-done), channel_id=1, source_target_pairs={{0,1},{1,2},{2,3},{3,4},{4,5},{5,6},{6,7},{7,8},{8,9},{9,10},{10,1... | collective-permute-start | bytes 196616 | tf_op jit(solution)/shard_map/ppermute | solution.py:86
  80.7 7.6 %collective-permute-start.3 = (bf16[16,2048]{1,0:T(8,128)(2,1)S(1)}, bf16[16,2048]{1,0:T(8,128)(2,1)S(1)}, u32[]{:S(2)}, u32[]{:S(2)}) collective-permute-start(bf16[16,2048]{1,0:T(8,128)(2,1)S(1)} %collective-permute-done.1), channel_id=1, source_target_pairs={{0,15},{1,0},{2,1},{3,2},{4,3},{5,4},{6,5},{7,6},{8,7},{9,8},{10,9... | collective-permute-start | bytes 196616 | tf_op jit(solution)/shard_map/ppermute | solution.py:91
  88.2 8.0 %collective-permute-start.4 = (bf16[16,2048]{1,0:T(8,128)(2,1)S(1)}, bf16[16,2048]{1,0:T(8,128)(2,1)S(1)}, u32[]{:S(2)}, u32[]{:S(2)}) collective-permute-start(bf16[16,2048]{1,0:T(8,128)(2,1)S(1)} %collective-permute-done.2), channel_id=1, source_target_pairs={{0,1},{1,2},{2,3},{3,4},{4,5},{5,6},{6,7},{7,8},{8,9},{9,10},{10,1... | collective-permute-start | bytes 196616 | tf_op jit(solution)/shard_map/ppermute | solution.py:86
  88.3 8.0 %collective-permute-start.5 = (bf16[16,2048]{1,0:T(8,128)(2,1)S(1)}, bf16[16,2048]{1,0:T(8,128)(2,1)S(1)}, u32[]{:S(2)}, u32[]{:S(2)}) collective-permute-start(bf16[16,2048]{1,0:T(8,128)(2,1)S(1)} %collective-permute-done.3), channel_id=1, source_target_pairs={{0,15},{1,0},{2,1},{3,2},{4,3},{5,4},{6,5},{7,6},{8,7},{9,8},{10,9... | collective-permute-start | bytes 196616 | tf_op jit(solution)/shard_map/ppermute | solution.py:91
  96.2 7.6 %collective-permute-start.6 = (bf16[16,2048]{1,0:T(8,128)(2,1)S(1)}, bf16[16,2048]{1,0:T(8,128)(2,1)S(1)}, u32[]{:S(2)}, u32[]{:S(2)}) collective-permute-start(bf16[16,2048]{1,0:T(8,128)(2,1)S(1)} %collective-permute-done.4), channel_id=1, source_target_pairs={{0,1},{1,2},{2,3},{3,4},{4,5},{5,6},{6,7},{7,8},{8,9},{9,10},{10,1... | collective-permute-start | bytes 196616 | tf_op jit(solution)/shard_map/ppermute | solution.py:86
  96.2 7.6 %collective-permute-start.7 = (bf16[16,2048]{1,0:T(8,128)(2,1)S(1)}, bf16[16,2048]{1,0:T(8,128)(2,1)S(1)}, u32[]{:S(2)}, u32[]{:S(2)}) collective-permute-start(bf16[16,2048]{1,0:T(8,128)(2,1)S(1)} %collective-permute-done.5), channel_id=1, source_target_pairs={{0,15},{1,0},{2,1},{3,2},{4,3},{5,4},{6,5},{7,6},{8,7},{9,8},{10,9... | collective-permute-start | bytes 196616 | tf_op jit(solution)/shard_map/ppermute | solution.py:91
  103.8 7.6 %collective-permute-start.8 = (bf16[16,2048]{1,0:T(8,128)(2,1)S(1)}, bf16[16,2048]{1,0:T(8,128)(2,1)S(1)}, u32[]{:S(2)}, u32[]{:S(2)}) collective-permute-start(bf16[16,2048]{1,0:T(8,128)(2,1)S(1)} %collective-permute-done.6), channel_id=1, source_target_pairs={{0,1},{1,2},{2,3},{3,4},{4,5},{5,6},{6,7},{7,8},{8,9},{9,10},{10,1... | collective-permute-start | bytes 196616 | tf_op jit(solution)/shard_map/ppermute | solution.py:86
  103.8 7.6 %collective-permute-start.9 = (bf16[16,2048]{1,0:T(8,128)(2,1)S(1)}, bf16[16,2048]{1,0:T(8,128)(2,1)S(1)}, u32[]{:S(2)}, u32[]{:S(2)}) collective-permute-start(bf16[16,2048]{1,0:T(8,128)(2,1)S(1)} %collective-permute-done.7), channel_id=1, source_target_pairs={{0,15},{1,0},{2,1},{3,2},{4,3},{5,4},{6,5},{7,6},{8,7},{9,8},{10,9... | collective-permute-start | bytes 196616 | tf_op jit(solution)/shard_map/ppermute | solution.py:91
  111.4 7.6 %collective-permute-start.10 = (bf16[16,2048]{1,0:T(8,128)(2,1)S(1)}, bf16[16,2048]{1,0:T(8,128)(2,1)S(1)}, u32[]{:S(2)}, u32[]{:S(2)}) collective-permute-start(bf16[16,2048]{1,0:T(8,128)(2,1)S(1)} %collective-permute-done.8), channel_id=1, source_target_pairs={{0,1},{1,2},{2,3},{3,4},{4,5},{5,6},{6,7},{7,8},{8,9},{9,10},{10,1... | collective-permute-start | bytes 196616 | tf_op jit(solution)/shard_map/ppermute | solution.py:86
  111.4 7.6 %collective-permute-start.11 = (bf16[16,2048]{1,0:T(8,128)(2,1)S(1)}, bf16[16,2048]{1,0:T(8,128)(2,1)S(1)}, u32[]{:S(2)}, u32[]{:S(2)}) collective-permute-start(bf16[16,2048]{1,0:T(8,128)(2,1)S(1)} %collective-permute-done.9), channel_id=1, source_target_pairs={{0,15},{1,0},{2,1},{3,2},{4,3},{5,4},{6,5},{7,6},{8,7},{9,8},{10,9... | collective-permute-start | bytes 196616 | tf_op jit(solution)/shard_map/ppermute | solution.py:91
  119.0 7.6 %collective-permute-start.12 = (bf16[16,2048]{1,0:T(8,128)(2,1)S(1)}, bf16[16,2048]{1,0:T(8,128)(2,1)S(1)}, u32[]{:S(2)}, u32[]{:S(2)}) collective-permute-start(bf16[16,2048]{1,0:T(8,128)(2,1)S(1)} %collective-permute-done.10), channel_id=1, source_target_pairs={{0,1},{1,2},{2,3},{3,4},{4,5},{5,6},{6,7},{7,8},{8,9},{9,10},{10,1... | collective-permute-start | bytes 196616 | tf_op jit(solution)/shard_map/ppermute | solution.py:86
  119.0 7.6 %collective-permute-start.13 = (bf16[16,2048]{1,0:T(8,128)(2,1)S(1)}, bf16[16,2048]{1,0:T(8,128)(2,1)S(1)}, u32[]{:S(2)}, u32[]{:S(2)}) collective-permute-start(bf16[16,2048]{1,0:T(8,128)(2,1)S(1)} %collective-permute-done.11), channel_id=1, source_target_pairs={{0,15},{1,0},{2,1},{3,2},{4,3},{5,4},{6,5},{7,6},{8,7},{9,8},{10,9... | collective-permute-start | bytes 196616 | tf_op jit(solution)/shard_map/ppermute | solution.py:91
  126.5 7.6 %collective-permute-start.14 = (bf16[16,2048]{1,0:T(8,128)(2,1)S(1)}, bf16[16,2048]{1,0:T(8,128)(2,1)S(1)}, u32[]{:S(2)}, u32[]{:S(2)}) collective-permute-start(bf16[16,2048]{1,0:T(8,128)(2,1)S(1)} %collective-permute-done.12), channel_id=1, source_target_pairs={{0,1},{1,2},{2,3},{3,4},{4,5},{5,6},{6,7},{7,8},{8,9},{9,10},{10,1... | collective-permute-start | bytes 196616 | tf_op jit(solution)/shard_map/ppermute | solution.py:86
  154.0 14.6 %all-to-all-start.1 = ((bf16[16,4,256]{2,1,0:T(4,128)(2,1)}), bf16[16,4,256]{2,1,0:T(4,128)(2,1)S(1)}, u32[]{:S(2)}, u32[]{:S(2)}) async-start(bf16[16,4,256]{2,1,0:T(4,128)(2,1)} %all_to_all.20), calls=%async_computation.2 | async-start | bytes 65536 | tf_op jit(solution)/shard_map/all_to_all | solution.py:102
  160.9 39.3 %all-gather.2.cloned.1.call-start = ((), (), s32[]{:S(2)}) async-start(), calls=%async_computation.7 | async-start | bytes 3145728 | tf_op jit(solution)/shard_map/all_gather | solution.py:134
  168.6 22.6 %copy-start.2 = (bf16[4,4096]{1,0:T(4,128)(2,1)}, bf16[4,4096]{1,0:T(4,128)(2,1)S(1)}, u32[]{:S(2)}) copy-start(bf16[4,4096]{1,0:T(4,128)(2,1)S(1)} %add_convert_fusion) | copy-start | bytes 98308
  191.2 43.0 %reduce-scatter.5.cloned.1.call-start = ((), (), s32[]{:S(2)}) async-start(), calls=%async_computation.8 | async-start | bytes 6291456 | tf_op jit(solution)/shard_map/reduce_scatter | solution.py:140
  200.3 6.2 %copy-start.7 = (bf16[256,4096]{1,0:T(8,128)(2,1)S(1)}, bf16[256,4096]{1,0:T(8,128)(2,1)}, u32[]{:S(2)}) copy-start(bf16[256,4096]{1,0:T(8,128)(2,1)} %all-gather.2.cloned.1.call-done) | copy-start | bytes 6291460
  236.0 32.1 %copy-start.6 = (f32[4,8]{1,0:T(4,128)S(1)}, f32[4,8]{1,0:T(4,128)}, u32[]{:S(2)}) copy-start(f32[4,8]{1,0:T(4,128)} %param.20) | copy-start | bytes 388
  237.5 29.4 %all-to-all-start.3 = ((bf16[64,2,4096]{2,1,0:T(2,128)(2,1)}), bf16[64,2,4096]{2,1,0:T(2,128)(2,1)S(1)}, u32[]{:S(2)}, u32[]{:S(2)}) async-start(bf16[64,2,4096]{2,1,0:T(2,128)(2,1)} %reshape.159), calls=%async_computation.5 | async-start | bytes 2097152 | tf_op jit(solution)/shard_map/all_to_all | solution.py:144
Sparse Core Ops, SparseCore 0:
  135.4 17.0 reduce-scatter.2
  191.3 8.9 all-gather.1
  218.0 16.1 reduce-scatter.4
